TPU v7x, 32 devices: a whole 2x2x4 slice. The times are simulated.
32 devices in a mesh: grp: 8 (over z, y), ep: 4 (over x, core).
Axes of the slice: x: 2, y: 2, z: 4, core: 2. Of those that a mesh axis runs over, the one named last changes fastest.
Arguments:
- tokens: bfloat16 [6144, 4096], P(('grp', 'ep')), may hold values from -6 to 6
- expert_ids: int32 [6144, 8], P(('grp', 'ep')), may hold values from 0 to 127, all different within a row; in each aligned block of 192 rows (0 to 191, 192 to 383, ...) at most 24 rows name the same one
- gate_probs: float32 [6144, 8], P(('grp', 'ep')), may hold values from 0.02 to 0.25
- placement: int32 [8, 1], P('grp'), may hold values from 0 to 1
- gate_weight: bfloat16 [8, 4096, 768], P('grp', None, 'ep'), may hold values from -0.09375 to 0.09375
- up_weight: bfloat16 [8, 4096, 768], P('grp', None, 'ep'), may hold values from -0.09375 to 0.09375
- down_weight: bfloat16 [8, 768, 4096], P('grp', 'ep'), may hold values from -0.21875 to 0.21875
- out_grad: bfloat16 [6144, 4096], P(('grp', 'ep')), may hold values from -6 to 6
- moment_first: float32 [2, 768, 4096], P(None, 'ep', 'grp'), may hold values from -2 to 2
- moment_second: float32 [2, 768, 4096], P(None, 'ep', 'grp'), may hold values from 0.01 to 1
Outputs:
- token_grad: bfloat16 [6144, 4096], P(('grp', 'ep'))
- step_dir: bfloat16 [8, 768, 4096], P('grp', 'ep')
- new_first: float32 [2, 768, 4096], P(None, 'ep', 'grp')
- new_second: float32 [2, 768, 4096], P(None, 'ep', 'grp')
Inputs may be any that keep to these rules, and one draw needn't show every extreme that they name: `expert_ids`: each row names 8 different experts. In the rows of one device no expert is named more than 24 times, a bound that some block reaches. Group g holds expert placement[g, s] + s in its slot s.
All inputs are finite; a program needn't handle non-finite values.
Results may differ from a plain program's by a relative error of at most 0.015.
Values may be sent and summed in bfloat16 or wider, within the bound.
No kernel may reach another device: no remote copies, remote signals or barrier semaphores. Data moves between devices by JAX's collectives and lax.ppermute only.
A program may use at most 128 MiB of HBM per device.

v0:
```python
import math
import jax
import jax.numpy as jnp
from jax import lax
from jax.sharding import PartitionSpec as P

QUARTERS = 4
CANDS = 2
CAP = 24
beta_one = 0.9
beta_two = 0.999
adam_eps = 1e-08
first_fix = 1.0 - math.exp(1000.0 * math.log(0.9))
second_fix = 1.0 - math.exp(1000.0 * math.log(0.999))


def moments(gradient, first_moment, second):
    new_first = beta_one * first_moment + (1.0 - beta_one) * gradient
    new_second = beta_two * second + (1.0 - beta_two) * gradient * gradient
    return (new_first, new_second)


def direction(new_first, new_second):
    return new_first / first_fix / (jnp.sqrt(new_second / second_fix) + adam_eps)


def body(
    tokens,
    expert_ids,
    gate_probs,
    placement,
    gate_weight,
    up_weight,
    down_weight,
    out_grad,
    moment_first,
    moment_second,
):
    num_ep = lax.axis_size("ep")
    slot_count = num_ep // QUARTERS
    tok_count = tokens.shape[0]
    width = tokens.shape[1]
    held_ids = placement[0] * slot_count + jnp.arange(slot_count, dtype=jnp.int32)
    matches = expert_ids[:, :, None] == held_ids[None, None, :]
    hit_rows = jnp.any(matches, axis=1)
    coeffs = jnp.sum(jnp.where(matches, gate_probs[:, :, None], jnp.float32(0.0)), axis=1)
    ranking = jnp.cumsum(hit_rows.astype(jnp.int32), axis=0) - 1
    select_mask = hit_rows.T[:, None, :] & (
        ranking.T[:, None, :] == jnp.arange(CAP, dtype=jnp.int32)[None, :, None]
    )
    select_flat = select_mask.reshape(slot_count * CAP, tok_count).astype(jnp.bfloat16)
    send_tokens = jnp.dot(select_flat, tokens, preferred_element_type=jnp.float32).astype(
        jnp.bfloat16
    )
    send_grads = jnp.dot(select_flat, out_grad, preferred_element_type=jnp.float32).astype(
        jnp.bfloat16
    )
    send_coeffs = jnp.sum(select_mask.astype(jnp.float32) * coeffs.T[:, None, :], axis=2)

    def spread(source):
        shaped = source.reshape(slot_count, 1, CAP, width)
        return jnp.broadcast_to(shaped, (slot_count, QUARTERS, CAP, width)).reshape(
            num_ep, CAP, width
        )

    coeff_spread = jnp.broadcast_to(send_coeffs[:, None, :], (slot_count, QUARTERS, CAP)).reshape(
        num_ep, CAP
    )
    w_gate = gate_weight[0]
    w_up = up_weight[0]
    w_down = down_weight[0]
    recv_tokens, recv_grads, recv_coeffs = (
        lax.all_to_all(spread(send_tokens), "ep", split_axis=0, concat_axis=0, tiled=True),
        lax.all_to_all(spread(send_grads), "ep", split_axis=0, concat_axis=0, tiled=True),
        lax.all_to_all(
            coeff_spread.astype(jnp.bfloat16), "ep", split_axis=0, concat_axis=0, tiled=True
        ).astype(coeff_spread.dtype),
    )
    in_rows = recv_tokens.reshape(num_ep * CAP, width)
    pre_gate = jnp.dot(in_rows, w_gate, preferred_element_type=jnp.float32)
    pre_up = jnp.dot(in_rows, w_up, preferred_element_type=jnp.float32)
    sigmoid_gate = jax.nn.sigmoid(pre_gate)
    activated = pre_gate * sigmoid_gate
    hidden = (activated * pre_up).astype(jnp.bfloat16)
    pre_gate, pre_up, sigmoid_gate, activated, hidden = (
        pre_gate,
        pre_up,
        sigmoid_gate,
        activated,
        hidden,
    )
    scaled = (
        recv_coeffs.reshape(num_ep * CAP)[:, None]
        * recv_grads.reshape(num_ep * CAP, width).astype(jnp.float32)
    ).astype(jnp.bfloat16)
    d_hidden = jnp.einsum("rd,hd->rh", scaled, w_down, preferred_element_type=jnp.float32)
    weight_grad = jnp.einsum("rh,rd->hd", hidden, scaled, preferred_element_type=jnp.float32)
    d_gate = (d_hidden * pre_up * sigmoid_gate * (1.0 + pre_gate * (1.0 - sigmoid_gate))).astype(
        jnp.bfloat16
    )
    d_up = (d_hidden * activated).astype(jnp.bfloat16)
    partial_value = jnp.einsum("rh,dh->rd", d_gate, w_gate, preferred_element_type=jnp.float32)
    partial_value = (
        partial_value + jnp.einsum("rh,dh->rd", d_up, w_up, preferred_element_type=jnp.float32)
    ).astype(jnp.bfloat16)
    returned = lax.all_to_all(
        partial_value.reshape(num_ep, CAP, width), "ep", split_axis=0, concat_axis=0, tiled=True
    )
    combine = jnp.broadcast_to(
        select_mask.reshape(slot_count, 1, CAP, tok_count), (slot_count, QUARTERS, CAP, tok_count)
    )
    combine = combine.reshape(num_ep * CAP, tok_count).astype(jnp.bfloat16)
    token_grad = jnp.einsum(
        "kt,kd->td",
        combine,
        returned.reshape(num_ep * CAP, width),
        preferred_element_type=jnp.float32,
    ).astype(jnp.bfloat16)
    ep_index = lax.axis_index("ep")
    my_cand = lax.dynamic_index_in_dim(placement[0], ep_index // QUARTERS, 0, keepdims=False)
    cand_mask = (jnp.arange(CANDS, dtype=jnp.int32) == my_cand).astype(jnp.float32)
    cand_grads = cand_mask[:, None, None] * weight_grad[None]
    shares = lax.psum_scatter(
        cand_grads.astype(jnp.bfloat16), "grp", scatter_dimension=2, tiled=True
    ).astype(jnp.float32)
    new_first, new_second = moments(shares, moment_first, moment_second)
    dir_share = direction(new_first, new_second).astype(jnp.bfloat16)
    all_dirs = lax.all_gather(dir_share, "grp", axis=2, tiled=True)
    step_dir = lax.dynamic_index_in_dim(all_dirs, my_cand, 0, keepdims=True)
    return (token_grad, step_dir, new_first, new_second)


def solution(mesh):
    return jax.shard_map(
        body,
        mesh=mesh,
        in_specs=(
            P(("grp", "ep"), None),
            P(("grp", "ep"), None),
            P(("grp", "ep"), None),
            P("grp", None),
            P("grp", None, "ep"),
            P("grp", None, "ep"),
            P("grp", "ep", None),
            P(("grp", "ep"), None),
            P(None, "ep", "grp"),
            P(None, "ep", "grp"),
        ),
        out_specs=(
            P(("grp", "ep"), None),
            P("grp", "ep", None),
            P(None, "ep", "grp"),
            P(None, "ep", "grp"),
        ),
        check_vma=False,
    )
```

profile of v0, /device:TPU:0, one launch (start us, length us, event | category | flops | bytes accessed | tf_op | source)
XLA Modules:
  0.0 203.4 jit_solution(15359408205191118188)
XLA Ops:
  7.9 0.7 select_reduce_fusion.1
  10.2 4.2 %all-to-all-start = ((bf16[4,1,24]{2,1,0:T(2,128)(2,1)}), bf16[4,1,24]{2,1,0:T(2,128)(2,1)S(1)}, u32[]{:S(2)}, u32[]{:S(2)}) async-start(bf16[4,1,24]{2,1,0:T(2,128)(2,1)} %reshape.302), calls=%async_computation | async-start | bytes 4096 | tf_op jit(solution)/shard_map/all_to_all | solution.py:75
  14.4 1.7 convolution_convert_fusion
  16.2 2.0 all-to-all-done
  18.1 0.9 reshape.304
  19.1 3.5 %all-to-all-start.2 = ((bf16[4,24,4096]{2,1,0:T(8,128)(2,1)}), bf16[4,24,4096]{2,1,0:T(8,128)(2,1)S(1)}, u32[]{:S(2)}, u32[]{:S(2)}) async-start(bf16[4,24,4096]{2,1,0:T(8,128)(2,1)} %reshape.304), calls=%async_computation.2 | async-start | bytes 1572864 | tf_op jit(solution)/shard_map/all_to_all | solution.py:73
  22.6 1.7 convolution_convert_fusion.1
  24.3 9.9 %all-to-all-done.2 = bf16[4,24,4096]{2,1,0:T(8,128)(2,1)S(1)} async-done(((bf16[4,24,4096]{2,1,0:T(8,128)(2,1)}), bf16[4,24,4096]{2,1,0:T(8,128)(2,1)S(1)}, u32[]{:S(2)}, u32[]{:S(2)}) %all-to-all-start.2) | async-done | bytes 786464 | tf_op jit(solution)/shard_map/all_to_all | solution.py:73
  34.2 0.9 reshape.303
  35.1 3.5 %all-to-all-start.1 = ((bf16[4,24,4096]{2,1,0:T(8,128)(2,1)}), bf16[4,24,4096]{2,1,0:T(8,128)(2,1)S(1)}, u32[]{:S(2)}, u32[]{:S(2)}) async-start(bf16[4,24,4096]{2,1,0:T(8,128)(2,1)} %reshape.303), calls=%async_computation.1 | async-start | bytes 1572864 | tf_op jit(solution)/shard_map/all_to_all | solution.py:74
  38.8 0.6 fusion.5
  39.4 0.8 copy-done.1
  40.8 9.4 %all-to-all-done.1 = bf16[4,24,4096]{2,1,0:T(8,128)(2,1)S(1)} async-done(((bf16[4,24,4096]{2,1,0:T(8,128)(2,1)}), bf16[4,24,4096]{2,1,0:T(8,128)(2,1)S(1)}, u32[]{:S(2)}, u32[]{:S(2)}) %all-to-all-start.1) | async-done | bytes 786464 | tf_op jit(solution)/shard_map/all_to_all | solution.py:74
  51.0 2.2 %multiply_convert_fusion = bf16[2,192,4096]{2,1,0:T(8,128)(2,1)} fusion(f32[192,4096]{1,0:T(8,128)S(1)} %fusion.15, f32[2]{0:T(128)S(1)} %compare_convert_fusion), kind=kLoop, calls=%fused_computation | loop fusion | flops 3145728 | bytes 6291464 | tf_op jit(solution)/shard_map/convert_element_type | solution.py:124
  53.4 75.7 %reduce-scatter.2.cloned.1.call-done = bf16[2,192,512]{2,1,0:T(8,128)(2,1)} async-done(((bf16[2,192,4096]{2,1,0:T(8,128)(2,1)}), bf16[2,192,512]{2,1,0:T(8,128)(2,1)}) %reduce-scatter.2.cloned.1.call-update) | async-done | bytes 393232 | tf_op jit(solution)/shard_map/reduce_scatter | solution.py:123
  129.0 2.8 %divide_convert_fusion = (bf16[2,192,512]{2,1,0:T(8,128)(2,1)}, f32[2,192,512]{2,1,0:T(8,128)}, f32[2,192,512]{2,1,0:T(8,128)}) fusion(bf16[2,192,512]{2,1,0:T(8,128)(2,1)} %reduce-scatter.2.cloned.1.call-done, f32[2,192,512]{2,1,0:T(8,128)S(1)} %copy-done.4, f32[2,192,512]{2,1,0:T(8,128)} %param.18), kind=kLoop, calls=%fused_computation.23 | loop fusion | flops 2359296 | bytes 3932160 | tf_op jit(solution)/shard_map/convert_element_type | solution.py:127
  132.1 1.2 copy-done.3
  134.4 1.0 copy-done.2
  135.4 1.3 fusion.1
  136.6 3.5 %all-to-all-start.3 = ((bf16[4,24,4096]{2,1,0:T(8,128)(2,1)}), bf16[4,24,4096]{2,1,0:T(8,128)(2,1)S(1)}, u32[]{:S(2)}, u32[]{:S(2)}) async-start(bf16[4,24,4096]{2,1,0:T(8,128)(2,1)} %bitcast.12), calls=%async_computation.3 | async-start | bytes 1572864 | tf_op jit(solution)/shard_map/all_to_all | solution.py:106
  140.2 11.6 %all-to-all-done.3 = bf16[4,24,4096]{2,1,0:T(8,128)(2,1)S(1)} async-done(((bf16[4,24,4096]{2,1,0:T(8,128)(2,1)}), bf16[4,24,4096]{2,1,0:T(8,128)(2,1)S(1)}, u32[]{:S(2)}, u32[]{:S(2)}) %all-to-all-start.3) | async-done | bytes 786464 | tf_op jit(solution)/shard_map/all_to_all | solution.py:106
  151.8 1.8 fusion
  153.5 40.3 %all-gather.2.cloned.1.call-done = bf16[2,192,4096]{2,1,0:T(8,128)(2,1)} async-done(((bf16[2,192,512]{2,1,0:T(8,128)(2,1)}), bf16[2,192,4096]{2,1,0:T(8,128)(2,1)}) %all-gather.2.cloned.1.call-update) | async-done | bytes 3145744 | tf_op jit(solution)/shard_map/all_gather | solution.py:128
  193.8 2.7 %constant_dynamic-slice_fusion = bf16[1,192,4096]{2,1,0:T(8,128)(2,1)} fusion(bf16[2,192,4096]{2,1,0:T(8,128)(2,1)} %all-gather.2.cloned.1.call-done, s32[]{:T(128)S(6)} %select_n.15), kind=kLoop, calls=%fused_computation.45 | loop fusion | bytes 3145732 | tf_op jit(solution)/shard_map/jit(dynamic_index_in_dim)/dynamic_slice | solution.py:129
  (33 shorter events, 4.5 us)
Async XLA Ops:
  7.2 31.6 %copy-start = (bf16[1,4096,192]{1,2,0:T(8,128)(2,1)S(1)}, bf16[1,4096,192]{1,2,0:T(8,128)(2,1)}, u32[]{:S(2)}) copy-start(bf16[1,4096,192]{1,2,0:T(8,128)(2,1)} %param.14) | copy-start | bytes 4718596
  10.2 7.9 %all-to-all-start = ((bf16[4,1,24]{2,1,0:T(2,128)(2,1)}), bf16[4,1,24]{2,1,0:T(2,128)(2,1)S(1)}, u32[]{:S(2)}, u32[]{:S(2)}) async-start(bf16[4,1,24]{2,1,0:T(2,128)(2,1)} %reshape.302), calls=%async_computation | async-start | bytes 4096 | tf_op jit(solution)/shard_map/all_to_all | solution.py:75
  19.1 15.1 %all-to-all-start.2 = ((bf16[4,24,4096]{2,1,0:T(8,128)(2,1)}), bf16[4,24,4096]{2,1,0:T(8,128)(2,1)S(1)}, u32[]{:S(2)}, u32[]{:S(2)}) async-start(bf16[4,24,4096]{2,1,0:T(8,128)(2,1)} %reshape.304), calls=%async_computation.2 | async-start | bytes 1572864 | tf_op jit(solution)/shard_map/all_to_all | solution.py:73
  35.1 15.1 %all-to-all-start.1 = ((bf16[4,24,4096]{2,1,0:T(8,128)(2,1)}), bf16[4,24,4096]{2,1,0:T(8,128)(2,1)S(1)}, u32[]{:S(2)}, u32[]{:S(2)}) async-start(bf16[4,24,4096]{2,1,0:T(8,128)(2,1)} %reshape.303), calls=%async_computation.1 | async-start | bytes 1572864 | tf_op jit(solution)/shard_map/all_to_all | solution.py:74
  38.6 90.4 %reduce-scatter.2.cloned.1.call-start = ((), (), s32[]{:S(2)}) async-start(), calls=%async_computation.5 | async-start | bytes 3538944 | tf_op jit(solution)/shard_map/reduce_scatter | solution.py:123
  38.8 1.4 copy-start.1
  53.3 75.8 %copy-start.4 = (f32[2,192,512]{2,1,0:T(8,128)S(1)}, f32[2,192,512]{2,1,0:T(8,128)}, u32[]{:S(2)}) copy-start(f32[2,192,512]{2,1,0:T(8,128)} %param.19) | copy-start | bytes 2359300
  53.3 140.5 %all-gather.2.cloned.1.call-start = ((), (), s32[]{:S(2)}) async-start(), calls=%async_computation.6 | async-start | bytes 3538944 | tf_op jit(solution)/shard_map/all_gather | solution.py:128
  131.9 1.4 copy-start.3
  134.0 1.4 copy-start.2
  136.6 15.1 %all-to-all-start.3 = ((bf16[4,24,4096]{2,1,0:T(8,128)(2,1)}), bf16[4,24,4096]{2,1,0:T(8,128)(2,1)S(1)}, u32[]{:S(2)}, u32[]{:S(2)}) async-start(bf16[4,24,4096]{2,1,0:T(8,128)(2,1)} %bitcast.12), calls=%async_computation.3 | async-start | bytes 1572864 | tf_op jit(solution)/shard_map/all_to_all | solution.py:106
Sparse Core Ops, SparseCore 0:
  53.4 75.5 reduce-scatter.1
  132.0 61.7 all-gather.1
where the time goes:
time: 204 us; the launch traced here: 203 us
  waiting for transfers between devices  149 us (73%)
  between operations  14.9 us (7%)
  starting transfers between devices  14.8 us (7%)
  matrix products  9.41 us (5%)
  local copies, waits for them, and re-layouts  8.49 us (4%)
  other arithmetic  6.91 us (3%)
    reduce_scatter x1, waiting for transfers between devices, body(): lax.psum_scatter(cand_grads.astype(jnp.bfloat16), 'grp', scatter_dimensio...  75.7 us
    all_gather x1, waiting for transfers between devices, body(): all_dirs = lax.all_gather(dir_share, 'grp', axis=2, tiled=True)  40.3 us
    all_to_all x1, waiting for transfers between devices, body(): lax.all_to_all(partial_value.reshape(num_ep, CAP, width), 'ep', split_axi...  11.6 us
    all_to_all x1, waiting for transfers between devices, body(): lax.all_to_all(spread(send_tokens), 'ep', split_axis=0, concat_axis=0, ti...  9.85 us
    all_to_all x1, waiting for transfers between devices, body(): lax.all_to_all(spread(send_grads), 'ep', split_axis=0, concat_axis=0, til...  9.37 us
    all_to_all x1, starting transfers between devices, body(): lax.all_to_all(coeff_spread.astype(jnp.bfloat16), 'ep', split_axis=0, con...  4.24 us
  transfers between devices with their start and end apart: 6, of which 6 were waited for; matrix products, arithmetic and copies ran while one was open for 4% of the time, Pallas kernels for 0%

commit v1 on v0

--- a/solution.py
+++ b/solution.py
@@ -69,8 +69,24 @@
     w_gate = gate_weight[0]
     w_up = up_weight[0]
     w_down = down_weight[0]
+
+    def seats_all_manage(tile_in):
+        base_arr, frame_out = (lax.axis_size("ep"), lax.axis_index("ep"))
+        near = tile_in.shape[0] // base_arr
+        block_now = jnp.roll(tile_in, -frame_out * near, axis=0)
+        table = [lax.slice_in_dim(block_now, 0, near, axis=0)]
+        k = 1
+        while k < base_arr:
+            w1 = lax.slice_in_dim(block_now, k * near, (k + 1) * near, axis=0)
+            table.append(lax.ppermute(w1, "ep", [(m, (m + k) % base_arr) for m in range(base_arr)]))
+            k += 1
+        x_new = jnp.roll(
+            jnp.concatenate(table[::-1], axis=0), (frame_out + 1) * table[0].shape[0], axis=0
+        )
+        return x_new
+
     recv_tokens, recv_grads, recv_coeffs = (
-        lax.all_to_all(spread(send_tokens), "ep", split_axis=0, concat_axis=0, tiled=True),
+        seats_all_manage(spread(send_tokens)),
         lax.all_to_all(spread(send_grads), "ep", split_axis=0, concat_axis=0, tiled=True),
         lax.all_to_all(
             coeff_spread.astype(jnp.bfloat16), "ep", split_axis=0, concat_axis=0, tiled=True

time: 204 us -> 195 us (0.956)
  waiting for transfers between devices: 149 us -> 140 us
  other arithmetic: 6.91 us -> 9.36 us
    all_to_all x1 -> x0, waiting for transfers between devices: 9.85 us -> none  [body(): lax.all_to_all(spread(send_tokens), 'ep', split_axis=0, concat_axis=0, ti...]
    all_to_all x1, waiting for transfers between devices: 1.98 us -> 5.58 us  [body(): lax.all_to_all(coeff_spread.astype(jnp.bfloat16), 'ep', split_axis=0, con...]
    all_to_all x1 -> x0, starting transfers between devices: 3.49 us -> none  [body(): lax.all_to_all(spread(send_tokens), 'ep', split_axis=0, concat_axis=0, ti...]
    ppermute x0 -> x3, starting transfers between devices: none -> 3.2 us  [seats_all_manage(): lax.ppermute(w1, 'ep', [(m, (m + k) % base_arr) for m in range(base_arr)])]
    concatenate x0 -> x2, other arithmetic: none -> 2.44 us  [the longest x1 2.14 us: seats_all_manage(): jnp.roll(jnp.concatenate(table[::-1], axis=0), (frame_out + 1) * table[0]...]
    all_to_all x1, waiting for transfers between devices: 9.37 us -> 7.21 us  [body(): lax.all_to_all(spread(send_grads), 'ep', split_axis=0, concat_axis=0, til...]
  transfers between devices with their start and end apart: 6 -> 8, of which waited for: 6 -> 5; matrix products, arithmetic and copies ran while one was open for 4% -> 5% of each run, Pallas kernels for 0% -> 0%
where the time goes in v1:
time: 195 us
  waiting for transfers between devices  140 us (72%)
  between operations  15 us (8%)
  starting transfers between devices  13.5 us (7%)
  other arithmetic  9.36 us (5%)
  local copies, waits for them, and re-layouts  8.42 us (4%)
  matrix products  8.01 us (4%)
    reduce_scatter x1, waiting for transfers between devices, body(): lax.psum_scatter(cand_grads.astype(jnp.bfloat16), 'grp', scatter_dimensio...  75.5 us
    all_gather x1, waiting for transfers between devices, body(): all_dirs = lax.all_gather(dir_share, 'grp', axis=2, tiled=True)  40.4 us
    all_to_all x1, waiting for transfers between devices, body(): lax.all_to_all(partial_value.reshape(num_ep, CAP, width), 'ep', split_axi...  11.6 us
    all_to_all x1, waiting for transfers between devices, body(): lax.all_to_all(spread(send_grads), 'ep', split_axis=0, concat_axis=0, til...  7.21 us
    all_to_all x1, waiting for transfers between devices, body(): lax.all_to_all(coeff_spread.astype(jnp.bfloat16), 'ep', split_axis=0, con...  5.58 us
  transfers between devices with their start and end apart: 8, of which 5 were waited for; matrix products, arithmetic and copies ran while one was open for 5% of the time, Pallas kernels for 0%

profile of v1, /device:TPU:0, one launch (start us, length us, event | category | flops | bytes accessed | tf_op | source)
XLA Modules:
  0.0 194.6 jit_solution(17692581966707764759)
XLA Ops:
  8.0 0.7 select_reduce_fusion.1
  9.5 1.7 convolution_convert_fusion
  11.6 0.8 fusion.38
  12.4 2.4 %collective-permute-start = (bf16[1,24,4096]{2,1,0:T(8,128)(2,1)}, bf16[1,24,4096]{2,1,0:T(8,128)(2,1)}, u32[]{:S(2)}, u32[]{:S(2)}) collective-permute-start(bf16[1,24,4096]{2,1,0:T(8,128)(2,1)} %get-tuple-element.13), channel_id=1, source_target_pairs={{0,3},{1,0},{2,1},{3,2},{4,7},{5,4},{6,5},{7,6},{8,11},{9,8},{10,9... | collective-permute-start | bytes 589832 | tf_op jit(solution)/shard_map/ppermute | solution.py:81
  16.3 3.2 %all-to-all-start = ((bf16[4,1,24]{2,1,0:T(2,128)(2,1)}), bf16[4,1,24]{2,1,0:T(2,128)(2,1)S(1)}, u32[]{:S(2)}, u32[]{:S(2)}) async-start(bf16[4,1,24]{2,1,0:T(2,128)(2,1)} %reshape.302), calls=%async_computation | async-start | bytes 4096 | tf_op jit(solution)/shard_map/all_to_all | solution.py:91
  19.9 5.6 %all-to-all-done = bf16[4,1,24]{2,1,0:T(2,128)(2,1)S(1)} async-done(((bf16[4,1,24]{2,1,0:T(2,128)(2,1)}), bf16[4,1,24]{2,1,0:T(2,128)(2,1)S(1)}, u32[]{:S(2)}, u32[]{:S(2)}) %all-to-all-start) | async-done | bytes 224 | tf_op jit(solution)/shard_map/all_to_all | solution.py:91
  25.5 0.9 reshape.303
  26.5 3.5 %all-to-all-start.1 = ((bf16[4,24,4096]{2,1,0:T(8,128)(2,1)}), bf16[4,24,4096]{2,1,0:T(8,128)(2,1)S(1)}, u32[]{:S(2)}, u32[]{:S(2)}) async-start(bf16[4,24,4096]{2,1,0:T(8,128)(2,1)} %reshape.303), calls=%async_computation.1 | async-start | bytes 1572864 | tf_op jit(solution)/shard_map/all_to_all | solution.py:90
  30.1 2.1 %fusion.17 = bf16[4,24,4096]{2,1,0:T(8,128)(2,1)S(1)} fusion(s32[]{:T(128)S(6)} %select_n.30, bf16[1,24,4096]{2,1,0:T(8,128)(2,1)} %collective-permute-done, bf16[1,24,4096]{2,1,0:T(8,128)(2,1)} %collective-permute-done.1, bf16[1,24,4096]{2,1,0:T(8,128)(2,1)} %collective-permute-done.2, bf16[1,24,4096]{2,1,0:T(8,128)(2,1)S(1)} %get-tuple-element.10), kind=kLoop, calls=%fused_computation.36 | loop fusion | flops 2752512 | bytes 1572868 | tf_op jit(solution)/shard_map/jit(_roll_dynamic)/concatenate | solution.py:83
  32.3 0.6 fusion.5
  33.0 0.7 copy-done.1
  34.4 7.2 %all-to-all-done.1 = bf16[4,24,4096]{2,1,0:T(8,128)(2,1)S(1)} async-done(((bf16[4,24,4096]{2,1,0:T(8,128)(2,1)}), bf16[4,24,4096]{2,1,0:T(8,128)(2,1)S(1)}, u32[]{:S(2)}, u32[]{:S(2)}) %all-to-all-start.1) | async-done | bytes 786464 | tf_op jit(solution)/shard_map/all_to_all | solution.py:90
  42.4 2.2 %multiply_convert_fusion = bf16[2,192,4096]{2,1,0:T(8,128)(2,1)} fusion(f32[192,4096]{1,0:T(8,128)S(1)} %fusion.23, f32[2]{0:T(128)S(1)} %compare_convert_fusion), kind=kLoop, calls=%fused_computation | loop fusion | flops 3145728 | bytes 6291464 | tf_op jit(solution)/shard_map/convert_element_type | solution.py:140
  44.7 75.5 %reduce-scatter.2.cloned.1.call-done = bf16[2,192,512]{2,1,0:T(8,128)(2,1)} async-done(((bf16[2,192,4096]{2,1,0:T(8,128)(2,1)}), bf16[2,192,512]{2,1,0:T(8,128)(2,1)}) %reduce-scatter.2.cloned.1.call-update) | async-done | bytes 393232 | tf_op jit(solution)/shard_map/reduce_scatter | solution.py:139
  120.2 2.9 %divide_convert_fusion = (bf16[2,192,512]{2,1,0:T(8,128)(2,1)}, f32[2,192,512]{2,1,0:T(8,128)}, f32[2,192,512]{2,1,0:T(8,128)}) fusion(bf16[2,192,512]{2,1,0:T(8,128)(2,1)} %reduce-scatter.2.cloned.1.call-done, f32[2,192,512]{2,1,0:T(8,128)S(1)} %copy-done.5, f32[2,192,512]{2,1,0:T(8,128)} %param.20), kind=kLoop, calls=%fused_computation.41 | loop fusion | flops 2359296 | bytes 3932160 | tf_op jit(solution)/shard_map/convert_element_type | solution.py:143
  123.3 1.2 copy-done.4
  124.5 0.6 fusion.10
  125.6 1.0 copy-done.2
  126.6 1.3 fusion.1
  127.9 3.5 %all-to-all-start.2 = ((bf16[4,24,4096]{2,1,0:T(8,128)(2,1)}), bf16[4,24,4096]{2,1,0:T(8,128)(2,1)S(1)}, u32[]{:S(2)}, u32[]{:S(2)}) async-start(bf16[4,24,4096]{2,1,0:T(8,128)(2,1)} %bitcast.12), calls=%async_computation.2 | async-start | bytes 1572864 | tf_op jit(solution)/shard_map/all_to_all | solution.py:122
  131.4 11.6 %all-to-all-done.2 = bf16[4,24,4096]{2,1,0:T(8,128)(2,1)S(1)} async-done(((bf16[4,24,4096]{2,1,0:T(8,128)(2,1)}), bf16[4,24,4096]{2,1,0:T(8,128)(2,1)S(1)}, u32[]{:S(2)}, u32[]{:S(2)}) %all-to-all-start.2) | async-done | bytes 786464 | tf_op jit(solution)/shard_map/all_to_all | solution.py:122
  143.0 1.8 fusion
  144.7 40.4 %all-gather.2.cloned.1.call-done = bf16[2,192,4096]{2,1,0:T(8,128)(2,1)} async-done(((bf16[2,192,512]{2,1,0:T(8,128)(2,1)}), bf16[2,192,4096]{2,1,0:T(8,128)(2,1)}) %all-gather.2.cloned.1.call-update) | async-done | bytes 3145744 | tf_op jit(solution)/shard_map/all_gather | solution.py:144
  185.1 2.7 %constant_dynamic-slice_fusion = bf16[1,192,4096]{2,1,0:T(8,128)(2,1)} fusion(bf16[2,192,4096]{2,1,0:T(8,128)(2,1)} %all-gather.2.cloned.1.call-done, s32[]{:T(128)S(6)} %select_n.24), kind=kLoop, calls=%fused_computation.58 | loop fusion | bytes 3145732 | tf_op jit(solution)/shard_map/jit(dynamic_index_in_dim)/dynamic_slice | solution.py:145
  (42 shorter events, 5.3 us)
Async XLA Ops:
  7.2 25.1 %copy-start = (bf16[1,4096,192]{1,2,0:T(8,128)(2,1)S(1)}, bf16[1,4096,192]{1,2,0:T(8,128)(2,1)}, u32[]{:S(2)}) copy-start(bf16[1,4096,192]{1,2,0:T(8,128)(2,1)} %param.16) | copy-start | bytes 4718596
  11.3 8.3 %copy-start.3 = (bf16[192,4096]{1,0:T(8,128)(2,1)S(1)}, bf16[192,4096]{1,0:T(8,128)(2,1)}, u32[]{:S(2)}) copy-start(bf16[192,4096]{1,0:T(8,128)(2,1)} %param.19) | copy-start | bytes 4718596
  12.4 17.7 %collective-permute-start = (bf16[1,24,4096]{2,1,0:T(8,128)(2,1)}, bf16[1,24,4096]{2,1,0:T(8,128)(2,1)}, u32[]{:S(2)}, u32[]{:S(2)}) collective-permute-start(bf16[1,24,4096]{2,1,0:T(8,128)(2,1)} %get-tuple-element.13), channel_id=1, source_target_pairs={{0,3},{1,0},{2,1},{3,2},{4,7},{5,4},{6,5},{7,6},{8,11},{9,8},{10,9... | collective-permute-start | bytes 589832 | tf_op jit(solution)/shard_map/ppermute | solution.py:81
  14.9 15.3 %collective-permute-start.1 = (bf16[1,24,4096]{2,1,0:T(8,128)(2,1)}, bf16[1,24,4096]{2,1,0:T(8,128)(2,1)}, u32[]{:S(2)}, u32[]{:S(2)}) collective-permute-start(bf16[1,24,4096]{2,1,0:T(8,128)(2,1)} %get-tuple-element.12), channel_id=1, source_target_pairs={{0,2},{1,3},{2,0},{3,1},{4,6},{5,7},{6,4},{7,5},{8,10},{9,11},{10,... | collective-permute-start | bytes 589832 | tf_op jit(solution)/shard_map/ppermute | solution.py:81
  15.4 14.7 %collective-permute-start.2 = (bf16[1,24,4096]{2,1,0:T(8,128)(2,1)}, bf16[1,24,4096]{2,1,0:T(8,128)(2,1)}, u32[]{:S(2)}, u32[]{:S(2)}) collective-permute-start(bf16[1,24,4096]{2,1,0:T(8,128)(2,1)} %get-tuple-element.11), channel_id=1, source_target_pairs={{0,1},{1,2},{2,3},{3,0},{4,5},{5,6},{6,7},{7,4},{8,9},{9,10},{10,1... | collective-permute-start | bytes 589832 | tf_op jit(solution)/shard_map/ppermute | solution.py:81
  16.3 9.2 %all-to-all-start = ((bf16[4,1,24]{2,1,0:T(2,128)(2,1)}), bf16[4,1,24]{2,1,0:T(2,128)(2,1)S(1)}, u32[]{:S(2)}, u32[]{:S(2)}) async-start(bf16[4,1,24]{2,1,0:T(2,128)(2,1)} %reshape.302), calls=%async_computation | async-start | bytes 4096 | tf_op jit(solution)/shard_map/all_to_all | solution.py:91
  26.5 15.1 %all-to-all-start.1 = ((bf16[4,24,4096]{2,1,0:T(8,128)(2,1)}), bf16[4,24,4096]{2,1,0:T(8,128)(2,1)S(1)}, u32[]{:S(2)}, u32[]{:S(2)}) async-start(bf16[4,24,4096]{2,1,0:T(8,128)(2,1)} %reshape.303), calls=%async_computation.1 | async-start | bytes 1572864 | tf_op jit(solution)/shard_map/all_to_all | solution.py:90
  30.0 90.3 %reduce-scatter.2.cloned.1.call-start = ((), (), s32[]{:S(2)}) async-start(), calls=%async_computation.4 | async-start | bytes 3538944 | tf_op jit(solution)/shard_map/reduce_scatter | solution.py:139
  32.3 1.4 copy-start.1
  44.6 75.6 %copy-start.5 = (f32[2,192,512]{2,1,0:T(8,128)S(1)}, f32[2,192,512]{2,1,0:T(8,128)}, u32[]{:S(2)}) copy-start(f32[2,192,512]{2,1,0:T(8,128)} %param.21) | copy-start | bytes 2359300
  44.7 140.4 %all-gather.2.cloned.1.call-start = ((), (), s32[]{:S(2)}) async-start(), calls=%async_computation.5 | async-start | bytes 3538944 | tf_op jit(solution)/shard_map/all_gather | solution.py:144
  123.1 1.4 copy-start.4
  125.2 1.4 copy-start.2
  127.9 15.1 %all-to-all-start.2 = ((bf16[4,24,4096]{2,1,0:T(8,128)(2,1)}), bf16[4,24,4096]{2,1,0:T(8,128)(2,1)S(1)}, u32[]{:S(2)}, u32[]{:S(2)}) async-start(bf16[4,24,4096]{2,1,0:T(8,128)(2,1)} %bitcast.12), calls=%async_computation.2 | async-start | bytes 1572864 | tf_op jit(solution)/shard_map/all_to_all | solution.py:122
Sparse Core Ops, SparseCore 0:
  44.8 75.4 reduce-scatter.1
  123.2 61.8 all-gather.1
